TPU v7x, 256 devices: a whole 4x4x8 slice. The times are simulated.
256 devices in a mesh: ty: 16 (over y, x_hi, core), tx: 16 (over z, x_lo).
Axes of the slice: x: 4 (x_hi: 2, x_lo: 2; x = x_hi * 2 + x_lo), y: 4, z: 8, core: 2. Of those that a mesh axis runs over, the one named last changes fastest.
Arguments:
- block_input: bfloat16 [1024, 768, 256], P('ty', 'tx'), may hold values from -6 to 6
- cotangent: bfloat16 [1024, 768, 256], P('ty', 'tx'), may hold values from -6 to 6
- tissue: int32 [64, 48], P('ty', 'tx'), may hold values 0 or 1
- dw_weight: float32 [49, 256], replicated, may hold values from -0.875 to 0.875
- dw_bias: float32 [256], replicated, may hold values from -3 to 3
- ln_gain: float32 [256], replicated, may hold values from 0.5 to 1.5
- ln_bias: float32 [256], replicated, may hold values from -3 to 3
- w_expand: bfloat16 [256, 1024], replicated, may hold values from -0.375 to 0.375
- b_expand: float32 [1024], replicated, may hold values from -3 to 3
- w_reduce: bfloat16 [1024, 256], replicated, may hold values from -0.1875 to 0.1875
- layer_scale: float32 [256], replicated, may hold values from 0.5 to 2
Outputs:
- grad_input: bfloat16 [1024, 768, 256], P('ty', 'tx')
- grad_dw: float32 [49, 256], replicated
- grad_expand: float32 [256, 1024], replicated
- grad_reduce: float32 [1024, 256], replicated
Inputs may be any that keep to these rules, and one draw needn't show every extreme that they name: 1 marks a tile with tissue.
All inputs are finite; a program needn't handle non-finite values. No bound on the sum of `tissue` on one device may be relied on, other than what follows from the above.
Results may differ from a plain program's by a relative error of at most 0.007.
Values may be sent and summed in bfloat16 or wider, within the bound.
No kernel may reach another device: no remote copies, remote signals or barrier semaphores. Data moves between devices by JAX's collectives and lax.ppermute only.
A program may use at most 256 MiB of HBM per device.

v0:
```python
import math
import jax
import jax.numpy as jnp
from jax import lax
from jax.sharding import PartitionSpec as P

TILE = 16


def with_halo(block, sides, width):
    for axis, dim in sides:
        count = lax.axis_size(axis)
        forward = [(i, i + 1) for i in range(count - 1)]
        backward = [(target, source) for source, target in forward]
        low = lax.ppermute(
            lax.slice_in_dim(block, block.shape[dim] - width, None, axis=dim), axis, forward
        )
        high = lax.ppermute(lax.slice_in_dim(block, 0, width, axis=dim), axis, backward)
        block = jnp.concatenate([low, block, high], axis=dim)
    return block


def depthwise(padded, kernel, rows, cols):
    total = jnp.zeros((rows, cols, padded.shape[2]), jnp.float32)
    for row_off in range(7):
        for col_off in range(7):
            window = padded[row_off : row_off + rows, col_off : col_off + cols].astype(jnp.float32)
            total = total + window * kernel[row_off * 7 + col_off]
    return total


def filter_grad(padded, grad, rows, cols):
    gradf = grad.astype(jnp.float32)
    taps = []
    for row_off in range(7):
        for col_off in range(7):
            window = padded[row_off : row_off + rows, col_off : col_off + cols].astype(jnp.float32)
            taps.append(jnp.sum(window * gradf, axis=(0, 1)))
    return jnp.stack(taps)


def branch_back(pre, masked, ln_gain, ln_bias, w_expand, b_expand, w_reduce, layer_scale):
    center = pre - jnp.mean(pre, axis=-1, keepdims=True)
    rstd = lax.rsqrt(jnp.mean(center * center, axis=-1, keepdims=True) + 1e-06)
    nhat = center * rstd
    normed = (nhat * ln_gain + ln_bias).astype(jnp.bfloat16)
    zvals = jnp.dot(normed, w_expand, preferred_element_type=jnp.float32) + b_expand
    cdf = 0.5 * (1.0 + jax.scipy.special.erf(zvals * 0.7071067811865476))
    hidden = (zvals * cdf).astype(jnp.bfloat16)
    go_vals = (layer_scale * masked.astype(jnp.float32)).astype(jnp.bfloat16)
    dhid = jnp.dot(go_vals, w_reduce.T, preferred_element_type=jnp.float32)
    slope = cdf + zvals * jnp.exp(-0.5 * zvals * zvals) * 0.3989422804014327
    dzvals = (dhid * slope).astype(jnp.bfloat16)
    dnorm = jnp.dot(dzvals, w_expand.T, preferred_element_type=jnp.float32) * ln_gain
    grad = rstd * (
        dnorm
        - jnp.mean(dnorm, axis=-1, keepdims=True)
        - nhat * jnp.mean(dnorm * nhat, axis=-1, keepdims=True)
    )
    return (grad.astype(jnp.bfloat16), hidden, normed, go_vals, dzvals)


def body(
    block_input,
    cotangent,
    tissue,
    dw_weight,
    dw_bias,
    ln_gain,
    ln_bias,
    w_expand,
    b_expand,
    w_reduce,
    layer_scale,
):
    rows, cols, chans = block_input.shape
    mask = jnp.repeat(jnp.repeat(tissue, TILE, axis=0), TILE, axis=1)
    masked = (cotangent.astype(jnp.float32) * mask[:, :, None].astype(jnp.float32)).astype(
        jnp.bfloat16
    )
    params = (ln_gain, ln_bias, w_expand, b_expand, w_reduce, layer_scale)
    input_pad = with_halo(block_input, (("ty", 0), ("tx", 1)), 3)
    pre = depthwise(input_pad, dw_weight, rows, cols) + dw_bias
    grad, hidden, normed, go_vals, dzvals = branch_back(
        pre.reshape(-1, chans), masked.reshape(-1, chans), *params
    )
    grad_core = grad.reshape(rows, cols, chans)
    grad_pad = with_halo(grad_core, (("ty", 0), ("tx", 1)), 3)
    factor = 1.0 / math.sqrt(rows * lax.axis_size("ty") * cols * lax.axis_size("tx"))
    local_reduce = jnp.dot(hidden.T, go_vals, preferred_element_type=jnp.float32)
    local_expand = jnp.dot(normed.T, dzvals, preferred_element_type=jnp.float32)
    local_dw = filter_grad(input_pad, grad_core, rows, cols)
    total_expand, total_reduce, total_dw = lax.psum(
        (local_expand, local_reduce, local_dw), ("ty", "tx")
    )
    result = cotangent.astype(jnp.float32) + depthwise(grad_pad, dw_weight[::-1], rows, cols)
    return (
        result.astype(jnp.bfloat16),
        total_dw * factor,
        total_expand * factor,
        total_reduce * factor,
    )


def solution(mesh):
    placed = (
        P("ty", "tx", None),
        P("ty", "tx", None),
        P("ty", "tx"),
        P(),
        P(),
        P(),
        P(),
        P(),
        P(),
        P(),
        P(),
    )
    return jax.shard_map(
        body,
        mesh=mesh,
        in_specs=placed,
        out_specs=(P("ty", "tx", None), P(), P(), P()),
        check_vma=False,
    )
```

profile of v0, /device:TPU:2, one launch (start us, length us, event | category | flops | bytes accessed | tf_op | source)
XLA Modules:
  0.0 527.7 jit_solution(16179048149840862890)
XLA Ops:
  9.5 3.0 collective-permute-start
  14.7 2.0 fusion.8
  16.7 1.6 fusion.132
  20.4 3.8 collective-permute-start.2
  24.2 2.0 collective-permute-start.3
  27.4 4.8 collective-permute-done.3
  32.2 61.1 %fusion.180 = (f32[64,48]{1,0:T(8,128)S(1)}, f32[64,48,256]{2,1,0:T(8,128)}) fusion(f32[256]{0:T(256)S(1)} %copy-done.23, f32[256]{0:T(256)S(1)} %bitcast.232, bf16[70,3,256]{2,1,0:T(4,128)(2,1)S(1)} %collective-permute-done.3, bf16[70,48,256]{2,1,0:T(8,128)(2,1)} %copy-done.4, f32[256]{0:T(256)S(1)} %bitcast.234, f32[256]{0:T(256)S(1)} %bitcast.140, ...), kind=kLoop, calls=%fused_computation.358 | loop fusion | flops 215479296 | bytes 16154624 | tf_op jit(solution)/shard_map/reduce_sum | solution.py:43
  93.5 2.8 multiply_reduce_fusion.1
  96.4 3.1 add_convert_fusion
  99.6 1.8 fusion.188
  101.4 5.5 %fusion.6 = f32[1024,256]{1,0:T(8,128)} fusion(bf16[3072,256]{1,0:T(8,128)(2,1)S(1)} %copy-done.12, f32[3072,1024]{1,0:T(8,128)S(1)} %fusion.188, f32[1024]{0:T(1024)S(1)} %copy-done.27), kind=kOutput, calls=%fused_computation.99 | convolution fusion | flops 1629487104 | bytes 15208448 | tf_op jit(solution)/shard_map/dot_general | solution.py:90
  106.9 7.0 %fusion.5 = bf16[3072,1024]{1,0:T(8,128)(2,1)S(1)} fusion(f32[3072,1024]{1,0:T(8,128)S(1)} %fusion.188, bf16[3072,256]{1,0:T(8,128)(2,1)S(1)} %copy-done.12, bf16[1024,256]{1,0:T(8,128)(2,1)S(1)} %copy-done.26, f32[1024]{0:T(1024)S(1)} %copy-done.27), kind=kOutput, calls=%fused_computation.96 | convolution fusion | flops 1645215744 | bytes 20975616 | tf_op jit(solution)/shard_map/dot_general | solution.py:51
  113.9 2.7 copy-done.9
  116.5 2.8 fusion.189
  119.3 6.2 %fusion.179 = (f32[3072]{0:T(1024)S(1)}, f32[3072]{0:T(1024)S(1)}, f32[3072,256]{1,0:T(8,128)S(1)}) fusion(f32[3072]{0:T(1024)S(1)} %rsqrt.12, f32[3072]{0:T(1024)S(1)} %div.16, f32[64,48,256]{2,1,0:T(8,128)} %get-tuple-element.64, f32[256]{0:T(256)S(1)} %copy-done.25, bf16[3072,1024]{1,0:T(8,128)(2,1)} %copy-done.9, bf16[256,1024]{1,0:T(8,128)(2,1)S(1)} %copy-done), kind=kOutput, calls=%fused_computation.357 | convolution fusion | flops 1615325184 | bytes 13157376 | tf_op jit(solution)/shard_map/dot_general | solution.py:54
  125.5 2.5 multiply_convert_fusion.2
  128.1 1.3 collective-permute-start.5
  129.4 3.8 collective-permute-start.4
  133.2 5.1 fusion.129
  138.3 6.0 %fusion.131 = (f32[256]{0:T(256)S(1)}, f32[256]{0:T(256)S(1)}, f32[256]{0:T(256)S(1)}, f32[256]{0:T(256)S(1)}, f32[256]{0:T(256)S(1)}, /*index=5*/f32[256]{0:T(2...) fusion(bf16[64,48,256]{2,1,0:T(8,128)(2,1)S(1)} %bitcast.127, bf16[70,3,256]{2,1,0:T(4,128)(2,1)S(1)} %collective-permute-done.3, ...), kind=kLoop, calls=%fused_computation.276 | loop fusion | flops 43251456 | bytes 3409920 | tf_op jit(solution)/shard_map/reduce_sum | solution.py:38
  144.3 6.4 %fusion.130 = (f32[256]{0:T(256)S(1)}, f32[256]{0:T(256)S(1)}, f32[256]{0:T(256)S(1)}, f32[256]{0:T(256)S(1)}, f32[256]{0:T(256)S(1)}, /*index=5*/f32[256]{0:T(2...) fusion(bf16[64,48,256]{2,1,0:T(8,128)(2,1)S(1)} %bitcast.128, bf16[70,3,256]{2,1,0:T(4,128)(2,1)S(1)} %collective-permute-done.3, ...), kind=kLoop, calls=%fused_computation.275 | loop fusion | flops 43251456 | bytes 3409920 | tf_op jit(solution)/shard_map/reduce_sum | solution.py:38
  150.6 5.0 fusion.126
  155.7 5.1 fusion.127
  161.7 84.7 %psum.21 = f32[49,256]{1,0:T(8,128)S(1)} all-reduce(f32[49,256]{1,0:T(8,128)S(1)} %stack.199), channel_id=1, replica_groups=mesh['ty'=16,'tx'=16] {'ty','tx'}, use_global_device_ids=true, to_apply=%region_53.0 | all-reduce | flops 12544 | bytes 100352 | tf_op jit(solution)/shard_map/psum | solution.py:93
  246.5 2.0 collective-permute-start.6
  248.5 3.9 collective-permute-start.7
  253.1 3.9 collective-permute-done.6
  257.0 2.6 maximum_maximum_fusion
  259.6 33.2 %fusion.9 = bf16[64,48,256]{2,1,0:T(8,128)(2,1)} fusion(bf16[64,48,256]{2,1,0:T(8,128)(2,1)} %param.12, bf16[64,48,256]{2,1,0:T(8,128)(2,1)} %bitcast.134, bf16[3,48,256]{2,1,0:T(8,128)(2,1)S(1)} %collective-permute-done.5, bf16[3,48,256]{2,1,0:T(8,128)(2,1)S(1)} %collective-permute-done.4, bf16[70,51,256]{2,1,0:T(8,128)(2,1)S(1)} %get-tuple-element.66, ...), kind=kLoop, calls=%fused_computation.154 | loop fusion | flops 121896960 | bytes 70976512 | tf_op jit(solution)/shard_map/convert_element_type | solution.py:98
  292.9 223.4 %all-reduce.3.cloned.1.call-done = (f32[256,1024]{1,0:T(8,128)}, f32[1024,256]{1,0:T(8,128)}) async-done(((f32[256,1024]{1,0:T(8,128)}, f32[1024,256]{1,0:T(8,128)}), (f32[256,1024]{1,0:T(8,128)}, f32[1024,256]{1,0:T(8,128)})) %all-reduce.3.cloned.1.call-update) | async-done | bytes 2097168 | tf_op jit(solution)/shard_map/psum | solution.py:93
  516.2 2.3 broadcast_multiply_fusion.1
  518.6 2.3 broadcast_multiply_fusion
  (88 shorter events, 9.5 us)
Async XLA Ops:
  7.2 92.4 %copy-start = (bf16[256,1024]{1,0:T(8,128)(2,1)S(1)}, bf16[256,1024]{1,0:T(8,128)(2,1)}, u32[]{:S(2)}) copy-start(bf16[256,1024]{1,0:T(8,128)(2,1)} %param.18) | copy-start | bytes 1572868
  7.2 9.5 %copy-start.22 = (f32[256]{0:T(256)S(1)}, f32[256]{0:T(256)}, u32[]{:S(2)}) copy-start(f32[256]{0:T(256)} %param.21) | copy-start | bytes 3076
  7.2 509.0 %all-reduce.3.cloned.1.call-start = ((), (), s32[]{:S(2)}) async-start(), calls=%async_computation | async-start | bytes 4194304 | tf_op jit(solution)/shard_map/psum | solution.py:93
  8.2 10.4 %collective-permute-start.1 = (bf16[3,48,256]{2,1,0:T(8,128)(2,1)S(1)}, bf16[3,48,256]{2,1,0:T(8,128)(2,1)S(1)}, u32[]{:S(2)}, u32[]{:S(2)}) collective-permute-start(bf16[3,48,256]{2,1,0:T(8,128)(2,1)S(1)} %get-tuple-element.76), channel_id=1, source_target_pairs={{16,0},{32,16},{48,32},{64,48},{80,64},{96,80},{112,96},{128,112},... | collective-permute-start | bytes 221192 | tf_op jit(solution)/shard_map/ppermute | solution.py:18
  9.5 8.8 %collective-permute-start = (bf16[3,48,256]{2,1,0:T(8,128)(2,1)S(1)}, bf16[3,48,256]{2,1,0:T(8,128)(2,1)S(1)}, u32[]{:S(2)}, u32[]{:S(2)}) collective-permute-start(bf16[3,48,256]{2,1,0:T(8,128)(2,1)S(1)} %get-tuple-element.77), channel_id=1, source_target_pairs={{0,16},{16,32},{32,48},{48,64},{64,80},{80,96},{96,112},{112,128},... | collective-permute-start | bytes 221192 | tf_op jit(solution)/shard_map/ppermute | solution.py:15
  14.6 3.6 copy-start.13
  14.6 3.7 copy-start.10
  18.3 13.9 %copy-start.23 = (f32[256]{0:T(256)S(1)}, f32[256]{0:T(256)}, u32[]{:S(2)}) copy-start(f32[256]{0:T(256)} %param.15) | copy-start | bytes 3076
  18.7 74.6 %copy-start.2 = (bf16[67,48,256]{2,1,0:T(8,128)(2,1)}, bf16[67,48,256]{2,1,0:T(8,128)(2,1)S(1)}, u32[]{:S(2)}) copy-start(bf16[67,48,256]{2,1,0:T(8,128)(2,1)S(1)} %get-tuple-element.80) | copy-start | bytes 4939780
  20.4 7.0 %collective-permute-start.2 = (bf16[70,3,256]{2,1,0:T(4,128)(2,1)S(1)}, bf16[70,3,256]{2,1,0:T(4,128)(2,1)S(1)}, u32[]{:S(2)}, u32[]{:S(2)}) collective-permute-start(bf16[70,3,256]{2,1,0:T(4,128)(2,1)S(1)} %get-tuple-element.69), channel_id=1, source_target_pairs={{0,1},{1,2},{2,3},{3,4},{4,5},{5,6},{6,7},{7,8},{8,9},{9,10},{10,1... | collective-permute-start | bytes 322568 | tf_op jit(solution)/shard_map/ppermute | solution.py:15
  24.2 8.0 %collective-permute-start.3 = (bf16[70,3,256]{2,1,0:T(4,128)(2,1)S(1)}, bf16[70,3,256]{2,1,0:T(4,128)(2,1)S(1)}, u32[]{:S(2)}, u32[]{:S(2)}) collective-permute-start(bf16[70,3,256]{2,1,0:T(4,128)(2,1)S(1)} %get-tuple-element.70), channel_id=1, source_target_pairs={{1,0},{2,1},{3,2},{4,3},{5,4},{6,5},{7,6},{8,7},{9,8},{10,9},{11,1... | collective-permute-start | bytes 322568 | tf_op jit(solution)/shard_map/ppermute | solution.py:18
  26.2 67.1 %copy-start.14 = (f32[1,256]{1,0:T(1,128)}, f32[1,256]{1,0:T(1,128)S(1)}, u32[]{:S(2)}) copy-start(f32[1,256]{1,0:T(1,128)S(1)} %get-tuple-element.123) | copy-start | bytes 3076
  26.3 67.1 %copy-start.15 = (f32[1,256]{1,0:T(1,128)}, f32[1,256]{1,0:T(1,128)S(1)}, u32[]{:S(2)}) copy-start(f32[1,256]{1,0:T(1,128)S(1)} %get-tuple-element.124) | copy-start | bytes 3076
  26.3 67.1 %copy-start.16 = (f32[1,256]{1,0:T(1,128)}, f32[1,256]{1,0:T(1,128)S(1)}, u32[]{:S(2)}) copy-start(f32[1,256]{1,0:T(1,128)S(1)} %get-tuple-element.125) | copy-start | bytes 3076
  26.3 67.1 %copy-start.17 = (f32[1,256]{1,0:T(1,128)}, f32[1,256]{1,0:T(1,128)S(1)}, u32[]{:S(2)}) copy-start(f32[1,256]{1,0:T(1,128)S(1)} %get-tuple-element.126) | copy-start | bytes 3076
  26.3 67.1 %copy-start.18 = (f32[1,256]{1,0:T(1,128)}, f32[1,256]{1,0:T(1,128)S(1)}, u32[]{:S(2)}) copy-start(f32[1,256]{1,0:T(1,128)S(1)} %get-tuple-element.127) | copy-start | bytes 3076
  26.3 67.1 %copy-start.19 = (f32[1,256]{1,0:T(1,128)}, f32[1,256]{1,0:T(1,128)S(1)}, u32[]{:S(2)}) copy-start(f32[1,256]{1,0:T(1,128)S(1)} %get-tuple-element.128) | copy-start | bytes 3076
  26.3 67.1 %copy-start.20 = (f32[1,256]{1,0:T(1,128)}, f32[1,256]{1,0:T(1,128)S(1)}, u32[]{:S(2)}) copy-start(f32[1,256]{1,0:T(1,128)S(1)} %get-tuple-element.129) | copy-start | bytes 3076
  26.3 67.1 %copy-start.21 = (f32[1,256]{1,0:T(1,128)}, f32[1,256]{1,0:T(1,128)S(1)}, u32[]{:S(2)}) copy-start(f32[1,256]{1,0:T(1,128)S(1)} %get-tuple-element.130) | copy-start | bytes 3076
  93.4 3.0 copy-start.24
  93.4 3.0 copy-start.25
  101.4 5.5 %copy-start.26 = (bf16[1024,256]{1,0:T(8,128)(2,1)S(1)}, bf16[1024,256]{1,0:T(8,128)(2,1)}, u32[]{:S(2)}) copy-start(bf16[1024,256]{1,0:T(8,128)(2,1)} %param.20) | copy-start | bytes 1572868
  119.3 6.2 %copy-start.8 = (f32[64,48,256]{2,1,0:T(8,128)S(1)}, f32[64,48,256]{2,1,0:T(8,128)}, u32[]{:S(2)}) copy-start(f32[64,48,256]{2,1,0:T(8,128)} %get-tuple-element.64) | copy-start | bytes 9437188
  125.5 7.6 %copy-start.5 = (bf16[70,48,256]{2,1,0:T(8,128)(2,1)S(1)}, bf16[70,48,256]{2,1,0:T(8,128)(2,1)}, u32[]{:S(2)}) copy-start(bf16[70,48,256]{2,1,0:T(8,128)(2,1)} %copy-done.4) | copy-start | bytes 5160964
  125.5 7.6 %copy-start.7 = (bf16[67,48,256]{2,1,0:T(8,128)(2,1)S(1)}, bf16[67,48,256]{2,1,0:T(8,128)(2,1)}, u32[]{:S(2)}) copy-start(bf16[67,48,256]{2,1,0:T(8,128)(2,1)} %copy-done.6) | copy-start | bytes 4939780
  125.5 7.6 %copy-start.11 = (bf16[64,48,256]{2,1,0:T(8,128)(2,1)S(1)}, bf16[64,48,256]{2,1,0:T(8,128)(2,1)}, u32[]{:S(2)}) copy-start(bf16[64,48,256]{2,1,0:T(8,128)(2,1)} %param.11) | copy-start | bytes 4718596
  128.1 118.4 %copy-start.1 = (bf16[3072,256]{1,0:T(8,128)(2,1)}, bf16[3072,256]{1,0:T(8,128)(2,1)S(1)}, u32[]{:S(2)}) copy-start(bf16[3072,256]{1,0:T(8,128)(2,1)S(1)} %multiply_convert_fusion.2) | copy-start | bytes 4718596
  128.1 118.3 %collective-permute-start.5 = (bf16[3,48,256]{2,1,0:T(8,128)(2,1)S(1)}, bf16[3,48,256]{2,1,0:T(8,128)(2,1)S(1)}, u32[]{:S(2)}, u32[]{:S(2)}) collective-permute-start(bf16[3,48,256]{2,1,0:T(8,128)(2,1)S(1)} %bitcast.137), channel_id=1, source_target_pairs={{16,0},{32,16},{48,32},{64,48},{80,64},{96,80},{112,96},{128,112},... | collective-permute-start | bytes 221192 | tf_op jit(solution)/shard_map/ppermute | solution.py:18
  129.4 117.0 %collective-permute-start.4 = (bf16[3,48,256]{2,1,0:T(8,128)(2,1)S(1)}, bf16[3,48,256]{2,1,0:T(8,128)(2,1)S(1)}, u32[]{:S(2)}, u32[]{:S(2)}) collective-permute-start(bf16[3,48,256]{2,1,0:T(8,128)(2,1)S(1)} %bitcast.136), channel_id=1, source_target_pairs={{0,16},{16,32},{32,48},{48,64},{64,80},{80,96},{96,112},{112,128},... | collective-permute-start | bytes 221192 | tf_op jit(solution)/shard_map/ppermute | solution.py:15
  150.6 10.1 %copy-start.3 = (bf16[67,48,256]{2,1,0:T(8,128)(2,1)S(1)}, bf16[67,48,256]{2,1,0:T(8,128)(2,1)}, u32[]{:S(2)}) copy-start(bf16[67,48,256]{2,1,0:T(8,128)(2,1)} %copy-done.2) | copy-start | bytes 4939780
  246.5 10.5 %collective-permute-start.6 = (bf16[70,3,256]{2,1,0:T(4,128)(2,1)S(1)}, bf16[70,3,256]{2,1,0:T(4,128)(2,1)S(1)}, u32[]{:S(2)}, u32[]{:S(2)}) collective-permute-start(bf16[70,3,256]{2,1,0:T(4,128)(2,1)S(1)} %get-tuple-element.67), channel_id=1, source_target_pairs={{0,1},{1,2},{2,3},{3,4},{4,5},{5,6},{6,7},{7,8},{8,9},{9,10},{10,1... | collective-permute-start | bytes 322568 | tf_op jit(solution)/shard_map/ppermute | solution.py:15
  248.5 8.5 %collective-permute-start.7 = (bf16[70,3,256]{2,1,0:T(4,128)(2,1)S(1)}, bf16[70,3,256]{2,1,0:T(4,128)(2,1)S(1)}, u32[]{:S(2)}, u32[]{:S(2)}) collective-permute-start(bf16[70,3,256]{2,1,0:T(4,128)(2,1)S(1)} %get-tuple-element.68), channel_id=1, source_target_pairs={{1,0},{2,1},{3,2},{4,3},{5,4},{6,5},{7,6},{8,7},{9,8},{10,9},{11,1... | collective-permute-start | bytes 322568 | tf_op jit(solution)/shard_map/ppermute | solution.py:18
  (5 other events, 9.3 us)
Sparse Core Ops, SparseCore 0:
  253.2 262.9 all-reduce.2
where the time goes:
time: 528 us
  waiting for transfers between devices  233 us (44%)
  other arithmetic  143 us (27%)
  blocking collectives  84.7 us (16%)
  matrix products  23.2 us (4%)
  starting transfers between devices  21.1 us (4%)
  between operations  14.7 us (3%)
  local copies, waits for them, and re-layouts  7.49 us (1%)
    psum x1, waiting for transfers between devices, body(): lax.psum((local_expand, local_reduce, local_dw), ('ty', 'tx'))  223 us
    psum x1, blocking collectives, body(): lax.psum((local_expand, local_reduce, local_dw), ('ty', 'tx'))  84.7 us
    reduce_sum x1, other arithmetic, branch_back(): center = pre - jnp.mean(pre, axis=-1, keepdims=True)  61.1 us
    convert_element_type x1, other arithmetic, body(): result.astype(jnp.bfloat16)  33.2 us
    reduce_sum x6, other arithmetic, filter_grad(): taps.append(jnp.sum(window * gradf, axis=(0, 1)))  28.4 us
    ppermute x4, starting transfers between devices, with_halo(): lax.ppermute(lax.slice_in_dim(block, block.shape[dim] - width, None, axis...  12.6 us
  transfers between devices with their start and end apart: 9, of which 4 were waited for; matrix products, arithmetic and copies ran while one was open for 13% of the time, Pallas kernels for 0%

commit v1 on v0

--- a/solution.py
+++ b/solution.py
@@ -5,6 +5,9 @@
 from jax.sharding import PartitionSpec as P
 
 TILE = 16
+mark_the_things = lambda field, row_axis, dev_axis: jax.lax.psum(
+    jax.lax.psum(field, row_axis), dev_axis
+)
 
 
 def with_halo(block, sides, width):
@@ -90,8 +93,8 @@
     local_reduce = jnp.dot(hidden.T, go_vals, preferred_element_type=jnp.float32)
     local_expand = jnp.dot(normed.T, dzvals, preferred_element_type=jnp.float32)
     local_dw = filter_grad(input_pad, grad_core, rows, cols)
-    total_expand, total_reduce, total_dw = lax.psum(
-        (local_expand, local_reduce, local_dw), ("ty", "tx")
+    total_expand, total_reduce, total_dw = mark_the_things(
+        (local_expand, local_reduce, local_dw), "ty", "tx"
     )
     result = cotangent.astype(jnp.float32) + depthwise(grad_pad, dw_weight[::-1], rows, cols)
     return (

time: 528 us -> 475 us (0.90)
  waiting for transfers between devices: 233 us -> 111 us
  blocking collectives: 84.7 us -> 131 us
  other arithmetic: 143 us -> 164 us
    psum x1 -> x2, waiting for transfers between devices: 223 us -> 101 us  [the longest x1 101 us: jax.lax.psum(jax.lax.psum(field, row_axis), dev_axis)]
    psum x1 -> x2, blocking collectives: 84.7 us -> 131 us  [the longest x1 68.4 us: jax.lax.psum(field, row_axis)]
    convert_element_type x1, other arithmetic: 33.2 us -> 44.3 us  [body(): result.astype(jnp.bfloat16)]
    reduce_sum x6, other arithmetic: 28.4 us -> 36.8 us  [filter_grad(): taps.append(jnp.sum(window * gradf, axis=(0, 1)))]
  transfers between devices with their start and end apart: 9 -> 10, of which waited for: 4 -> 5; matrix products, arithmetic and copies ran while one was open for 13% -> 19% of each run, Pallas kernels for 0% -> 0%
where the time goes in v1:
time: 475 us; the launch traced here: 473 us
  other arithmetic  164 us (35%)
  blocking collectives  131 us (28%)
  waiting for transfers between devices  111 us (23%)
  matrix products  23.2 us (5%)
  starting transfers between devices  21.9 us (5%)
  between operations  14.5 us (3%)
  local copies, waits for them, and re-layouts  7.46 us (2%)
    psum x1, waiting for transfers between devices, jax.lax.psum(jax.lax.psum(field, row_axis), dev_axis)  101 us
    psum x1, blocking collectives, jax.lax.psum(field, row_axis)  68.4 us
    psum x1, blocking collectives, jax.lax.psum(jax.lax.psum(field, row_axis), dev_axis)  62.8 us
    reduce_sum x1, other arithmetic, branch_back(): center = pre - jnp.mean(pre, axis=-1, keepdims=True)  61 us
    convert_element_type x1, other arithmetic, body(): result.astype(jnp.bfloat16)  44.3 us
    reduce_sum x6, other arithmetic, filter_grad(): taps.append(jnp.sum(window * gradf, axis=(0, 1)))  36.8 us
    ppermute x4, starting transfers between devices, with_halo(): lax.ppermute(lax.slice_in_dim(block, block.shape[dim] - width, None, axis...  14.7 us
  transfers between devices with their start and end apart: 10, of which 5 were waited for; matrix products, arithmetic and copies ran while one was open for 19% of the time, Pallas kernels for 0%

profile of v1, /device:TPU:2, one launch (start us, length us, event | category | flops | bytes accessed | tf_op | source)
XLA Modules:
  0.0 473.3 jit_solution(13476867056003845825)
XLA Ops:
  9.5 3.0 collective-permute-start
  14.7 2.0 fusion.8
  16.7 1.6 fusion.132
  20.4 3.8 collective-permute-start.2
  24.2 2.0 collective-permute-start.3
  27.4 4.8 %collective-permute-done.3 = bf16[70,3,256]{2,1,0:T(4,128)(2,1)S(1)} collective-permute-done((bf16[70,3,256]{2,1,0:T(4,128)(2,1)S(1)}, bf16[70,3,256]{2,1,0:T(4,128)(2,1)S(1)}, u32[]{:S(2)}, u32[]{:S(2)}) %collective-permute-start.3) | collective-permute-done | bytes 107552 | tf_op jit(solution)/shard_map/ppermute | solution.py:21
  32.2 61.0 %fusion.180 = (f32[64,48]{1,0:T(8,128)S(1)}, f32[64,48,256]{2,1,0:T(8,128)}) fusion(f32[256]{0:T(256)S(1)} %copy-done.15, f32[256]{0:T(256)S(1)} %bitcast.232, bf16[70,3,256]{2,1,0:T(4,128)(2,1)S(1)} %collective-permute-done.3, bf16[70,48,256]{2,1,0:T(8,128)(2,1)} %copy-done.4, f32[256]{0:T(256)S(1)} %bitcast.234, f32[256]{0:T(256)S(1)} %bitcast.140, ...), kind=kLoop, calls=%fused_computation.358 | loop fusion | flops 215479296 | bytes 16154624 | tf_op jit(solution)/shard_map/reduce_sum | solution.py:46
  93.3 2.8 multiply_reduce_fusion.1
  96.2 3.1 add_convert_fusion
  99.3 1.8 fusion.188
  101.2 5.5 %fusion.6 = f32[1024,256]{1,0:T(8,128)} fusion(bf16[3072,256]{1,0:T(8,128)(2,1)S(1)} %copy-done.12, f32[3072,1024]{1,0:T(8,128)S(1)} %fusion.188, f32[1024]{0:T(1024)S(1)} %copy-done.19), kind=kOutput, calls=%fused_computation.99 | convolution fusion | flops 1629487104 | bytes 15208448 | tf_op jit(solution)/shard_map/dot_general | solution.py:93
  106.7 7.0 %fusion.5 = bf16[3072,1024]{1,0:T(8,128)(2,1)S(1)} fusion(f32[3072,1024]{1,0:T(8,128)S(1)} %fusion.188, bf16[3072,256]{1,0:T(8,128)(2,1)S(1)} %copy-done.12, bf16[1024,256]{1,0:T(8,128)(2,1)S(1)} %copy-done.18, f32[1024]{0:T(1024)S(1)} %copy-done.19), kind=kOutput, calls=%fused_computation.96 | convolution fusion | flops 1645215744 | bytes 20975616 | tf_op jit(solution)/shard_map/dot_general | solution.py:54
  113.6 2.7 copy-done.9
  116.3 2.8 fusion.189
  119.1 6.2 %fusion.179 = (f32[3072]{0:T(1024)S(1)}, f32[3072]{0:T(1024)S(1)}, f32[3072,256]{1,0:T(8,128)S(1)}) fusion(f32[3072]{0:T(1024)S(1)} %rsqrt.12, f32[3072]{0:T(1024)S(1)} %div.16, f32[64,48,256]{2,1,0:T(8,128)} %get-tuple-element.66, f32[256]{0:T(256)S(1)} %copy-done.17, bf16[3072,1024]{1,0:T(8,128)(2,1)} %copy-done.9, bf16[256,1024]{1,0:T(8,128)(2,1)S(1)} %copy-done), kind=kOutput, calls=%fused_computation.357 | convolution fusion | flops 1615325184 | bytes 13157376 | tf_op jit(solution)/shard_map/dot_general | solution.py:57
  125.3 2.5 multiply_convert_fusion.2
  130.0 3.7 collective-permute-start.4
  133.8 14.4 %fusion.131 = (f32[256]{0:T(256)S(1)}, f32[256]{0:T(256)S(1)}, f32[256]{0:T(256)S(1)}, f32[256]{0:T(256)S(1)}, f32[256]{0:T(256)S(1)}, /*index=5*/f32[256]{0:T(2...) fusion(bf16[64,48,256]{2,1,0:T(8,128)(2,1)S(1)} %bitcast.127, bf16[70,3,256]{2,1,0:T(4,128)(2,1)S(1)} %collective-permute-done.3, ...), kind=kLoop, calls=%fused_computation.276 | loop fusion | flops 43251456 | bytes 3409920 | tf_op jit(solution)/shard_map/reduce_sum | solution.py:41
  148.2 6.4 %fusion.130 = (f32[256]{0:T(256)S(1)}, f32[256]{0:T(256)S(1)}, f32[256]{0:T(256)S(1)}, f32[256]{0:T(256)S(1)}, f32[256]{0:T(256)S(1)}, /*index=5*/f32[256]{0:T(2...) fusion(bf16[64,48,256]{2,1,0:T(8,128)(2,1)S(1)} %bitcast.128, bf16[70,3,256]{2,1,0:T(4,128)(2,1)S(1)} %collective-permute-done.3, ...), kind=kLoop, calls=%fused_computation.275 | loop fusion | flops 43251456 | bytes 3409920 | tf_op jit(solution)/shard_map/reduce_sum | solution.py:41
  154.6 5.0 %fusion.126 = (f32[256]{0:T(256)S(1)}, f32[256]{0:T(256)S(1)}, f32[256]{0:T(256)S(1)}, f32[256]{0:T(256)S(1)}, f32[256]{0:T(256)S(1)}, /*index=5*/f32[256]{0:T(2...) fusion(bf16[64,48,256]{2,1,0:T(8,128)(2,1)S(1)} %bitcast.129, bf16[70,48,256]{2,1,0:T(8,128)(2,1)S(1)} %copy-done.5, ...), kind=kLoop, calls=%fused_computation.271 | loop fusion | flops 43251456 | bytes 3409920 | tf_op jit(solution)/shard_map/reduce_sum | solution.py:41
  159.6 5.1 %fusion.127 = (f32[256]{0:T(256)S(1)}, f32[256]{0:T(256)S(1)}, f32[256]{0:T(256)S(1)}, f32[256]{0:T(256)S(1)}, f32[256]{0:T(256)S(1)}, /*index=5*/f32[256]{0:T(2...) fusion(bf16[64,48,256]{2,1,0:T(8,128)(2,1)S(1)} %bitcast.130, bf16[70,48,256]{2,1,0:T(8,128)(2,1)S(1)} %copy-done.5, ...), kind=kLoop, calls=%fused_computation.272 | loop fusion | flops 43251456 | bytes 3409920 | tf_op jit(solution)/shard_map/reduce_sum | solution.py:41
  164.7 5.1 %fusion.129 = (f32[256]{0:T(256)S(1)}, f32[256]{0:T(256)S(1)}, f32[256]{0:T(256)S(1)}, f32[256]{0:T(256)S(1)}, f32[256]{0:T(256)S(1)}, /*index=5*/f32[256]{0:T(2...) fusion(bf16[64,48,256]{2,1,0:T(8,128)(2,1)S(1)} %bitcast.131, ...), kind=kLoop, calls=%fused_computation.274 | loop fusion | flops 38532608 | bytes 9809920 | tf_op jit(solution)/shard_map/reduce_sum | solution.py:41
  170.0 68.4 %psum.42 = f32[49,256]{1,0:T(8,128)S(1)} all-reduce(f32[49,256]{1,0:T(8,128)S(1)} %stack.199), channel_id=1, replica_groups=mesh['ty'=16,'tx'=16] {'ty'}, use_global_device_ids=true, to_apply=%region_53.0 | all-reduce | flops 12544 | bytes 100352 | tf_op jit(solution)/shard_map/psum | solution.py:9
  238.4 62.8 %psum.43 = f32[49,256]{1,0:T(8,128)S(1)} all-reduce(f32[49,256]{1,0:T(8,128)S(1)} %psum.42), channel_id=1, replica_groups=mesh['ty'=16,'tx'=16] {'tx'}, use_global_device_ids=true, to_apply=%region_54.0 | all-reduce | flops 12544 | bytes 100352 | tf_op jit(solution)/shard_map/psum | solution.py:8
  301.3 4.2 collective-permute-start.6
  305.5 2.5 collective-permute-start.7
  309.1 4.2 collective-permute-done.7
  313.4 3.5 maximum_maximum_fusion
  316.9 44.3 %fusion.9 = bf16[64,48,256]{2,1,0:T(8,128)(2,1)} fusion(bf16[64,48,256]{2,1,0:T(8,128)(2,1)} %param.12, bf16[64,48,256]{2,1,0:T(8,128)(2,1)} %bitcast.134, bf16[3,48,256]{2,1,0:T(8,128)(2,1)S(1)} %collective-permute-done.5, bf16[3,48,256]{2,1,0:T(8,128)(2,1)S(1)} %collective-permute-done.4, bf16[70,51,256]{2,1,0:T(8,128)(2,1)} %get-tuple-element.68, ...), kind=kLoop, calls=%fused_computation.154 | loop fusion | flops 121896960 | bytes 70976512 | tf_op jit(solution)/shard_map/convert_element_type | solution.py:101
  361.2 100.7 %all-reduce.5.cloned.1.call-done = (f32[256,1024]{1,0:T(8,128)}, f32[1024,256]{1,0:T(8,128)}) async-done(((f32[256,1024]{1,0:T(8,128)}, f32[1024,256]{1,0:T(8,128)}), (f32[256,1024]{1,0:T(8,128)}, f32[1024,256]{1,0:T(8,128)})) %all-reduce.5.cloned.1.call-update) | async-done | bytes 2097168 | tf_op jit(solution)/shard_map/psum | solution.py:8
  461.8 2.3 broadcast_multiply_fusion.1
  464.2 2.3 broadcast_multiply_fusion
  (76 shorter events, 11.4 us)
Async XLA Ops:
  7.2 92.1 %copy-start = (bf16[256,1024]{1,0:T(8,128)(2,1)S(1)}, bf16[256,1024]{1,0:T(8,128)(2,1)}, u32[]{:S(2)}) copy-start(bf16[256,1024]{1,0:T(8,128)(2,1)} %param.18) | copy-start | bytes 1572868
  7.2 9.5 %copy-start.14 = (f32[256]{0:T(256)S(1)}, f32[256]{0:T(256)}, u32[]{:S(2)}) copy-start(f32[256]{0:T(256)} %param.21) | copy-start | bytes 3076
  7.2 309.7 %all-reduce.7.cloned.1.call-start = ((), (), s32[]{:S(2)}) async-start(), calls=%async_computation.1 | async-start | bytes 4194304 | tf_op jit(solution)/shard_map/psum | solution.py:9
  8.2 10.4 %collective-permute-start.1 = (bf16[3,48,256]{2,1,0:T(8,128)(2,1)S(1)}, bf16[3,48,256]{2,1,0:T(8,128)(2,1)S(1)}, u32[]{:S(2)}, u32[]{:S(2)}) collective-permute-start(bf16[3,48,256]{2,1,0:T(8,128)(2,1)S(1)} %get-tuple-element.78), channel_id=1, source_target_pairs={{16,0},{32,16},{48,32},{64,48},{80,64},{96,80},{112,96},{128,112},... | collective-permute-start | bytes 221192 | tf_op jit(solution)/shard_map/ppermute | solution.py:21
  9.5 8.8 %collective-permute-start = (bf16[3,48,256]{2,1,0:T(8,128)(2,1)S(1)}, bf16[3,48,256]{2,1,0:T(8,128)(2,1)S(1)}, u32[]{:S(2)}, u32[]{:S(2)}) collective-permute-start(bf16[3,48,256]{2,1,0:T(8,128)(2,1)S(1)} %get-tuple-element.79), channel_id=1, source_target_pairs={{0,16},{16,32},{32,48},{48,64},{64,80},{80,96},{96,112},{112,128},... | collective-permute-start | bytes 221192 | tf_op jit(solution)/shard_map/ppermute | solution.py:18
  14.6 3.6 copy-start.13
  14.6 3.7 copy-start.10
  18.3 13.9 %copy-start.15 = (f32[256]{0:T(256)S(1)}, f32[256]{0:T(256)}, u32[]{:S(2)}) copy-start(f32[256]{0:T(256)} %param.15) | copy-start | bytes 3076
  18.6 1.7 copy-start.6
  18.7 1.2 copy-start.4
  18.7 74.5 %copy-start.2 = (bf16[67,48,256]{2,1,0:T(8,128)(2,1)}, bf16[67,48,256]{2,1,0:T(8,128)(2,1)S(1)}, u32[]{:S(2)}) copy-start(bf16[67,48,256]{2,1,0:T(8,128)(2,1)S(1)} %get-tuple-element.82) | copy-start | bytes 4939780
  20.4 7.0 %collective-permute-start.2 = (bf16[70,3,256]{2,1,0:T(4,128)(2,1)S(1)}, bf16[70,3,256]{2,1,0:T(4,128)(2,1)S(1)}, u32[]{:S(2)}, u32[]{:S(2)}) collective-permute-start(bf16[70,3,256]{2,1,0:T(4,128)(2,1)S(1)} %get-tuple-element.71), channel_id=1, source_target_pairs={{0,1},{1,2},{2,3},{3,4},{4,5},{5,6},{6,7},{7,8},{8,9},{9,10},{10,1... | collective-permute-start | bytes 322568 | tf_op jit(solution)/shard_map/ppermute | solution.py:18
  24.2 8.0 %collective-permute-start.3 = (bf16[70,3,256]{2,1,0:T(4,128)(2,1)S(1)}, bf16[70,3,256]{2,1,0:T(4,128)(2,1)S(1)}, u32[]{:S(2)}, u32[]{:S(2)}) collective-permute-start(bf16[70,3,256]{2,1,0:T(4,128)(2,1)S(1)} %get-tuple-element.72), channel_id=1, source_target_pairs={{1,0},{2,1},{3,2},{4,3},{5,4},{6,5},{7,6},{8,7},{9,8},{10,9},{11,1... | collective-permute-start | bytes 322568 | tf_op jit(solution)/shard_map/ppermute | solution.py:21
  93.2 3.0 copy-start.16
  93.2 3.0 copy-start.17
  99.3 1.8 copy-start.12
  99.3 1.8 copy-start.19
  101.2 5.5 %copy-start.18 = (bf16[1024,256]{1,0:T(8,128)(2,1)S(1)}, bf16[1024,256]{1,0:T(8,128)(2,1)}, u32[]{:S(2)}) copy-start(bf16[1024,256]{1,0:T(8,128)(2,1)} %param.20) | copy-start | bytes 1572868
  113.6 2.7 copy-start.9
  119.1 6.2 %copy-start.8 = (f32[64,48,256]{2,1,0:T(8,128)S(1)}, f32[64,48,256]{2,1,0:T(8,128)}, u32[]{:S(2)}) copy-start(f32[64,48,256]{2,1,0:T(8,128)} %get-tuple-element.66) | copy-start | bytes 9437188
  125.3 2.6 copy-start.3
  127.8 173.4 %copy-start.1 = (bf16[3072,256]{1,0:T(8,128)(2,1)}, bf16[3072,256]{1,0:T(8,128)(2,1)S(1)}, u32[]{:S(2)}) copy-start(bf16[3072,256]{1,0:T(8,128)(2,1)S(1)} %multiply_convert_fusion.2) | copy-start | bytes 4718596
  128.7 172.5 %collective-permute-start.5 = (bf16[3,48,256]{2,1,0:T(8,128)(2,1)S(1)}, bf16[3,48,256]{2,1,0:T(8,128)(2,1)S(1)}, u32[]{:S(2)}, u32[]{:S(2)}) collective-permute-start(bf16[3,48,256]{2,1,0:T(8,128)(2,1)S(1)} %bitcast.137), channel_id=1, source_target_pairs={{16,0},{32,16},{48,32},{64,48},{80,64},{96,80},{112,96},{128,112},... | collective-permute-start | bytes 221192 | tf_op jit(solution)/shard_map/ppermute | solution.py:21
  130.0 171.2 %collective-permute-start.4 = (bf16[3,48,256]{2,1,0:T(8,128)(2,1)S(1)}, bf16[3,48,256]{2,1,0:T(8,128)(2,1)S(1)}, u32[]{:S(2)}, u32[]{:S(2)}) collective-permute-start(bf16[3,48,256]{2,1,0:T(8,128)(2,1)S(1)} %bitcast.136), channel_id=1, source_target_pairs={{0,16},{16,32},{32,48},{48,64},{64,80},{80,96},{96,112},{112,128},... | collective-permute-start | bytes 221192 | tf_op jit(solution)/shard_map/ppermute | solution.py:18
  133.7 328.2 %all-reduce.5.cloned.1.call-start = ((), (), s32[]{:S(2)}) async-start(), calls=%async_computation | async-start | bytes 4194304 | tf_op jit(solution)/shard_map/psum | solution.py:8
  133.7 14.4 %copy-start.5 = (bf16[70,48,256]{2,1,0:T(8,128)(2,1)S(1)}, bf16[70,48,256]{2,1,0:T(8,128)(2,1)}, u32[]{:S(2)}) copy-start(bf16[70,48,256]{2,1,0:T(8,128)(2,1)} %copy-done.4) | copy-start | bytes 5160964
  154.6 10.1 %copy-start.7 = (bf16[67,48,256]{2,1,0:T(8,128)(2,1)S(1)}, bf16[67,48,256]{2,1,0:T(8,128)(2,1)}, u32[]{:S(2)}) copy-start(bf16[67,48,256]{2,1,0:T(8,128)(2,1)} %copy-done.6) | copy-start | bytes 4939780
  154.6 10.1 %copy-start.11 = (bf16[64,48,256]{2,1,0:T(8,128)(2,1)S(1)}, bf16[64,48,256]{2,1,0:T(8,128)(2,1)}, u32[]{:S(2)}) copy-start(bf16[64,48,256]{2,1,0:T(8,128)(2,1)} %param.11) | copy-start | bytes 4718596
  301.3 7.9 %collective-permute-start.6 = (bf16[70,3,256]{2,1,0:T(4,128)(2,1)S(1)}, bf16[70,3,256]{2,1,0:T(4,128)(2,1)S(1)}, u32[]{:S(2)}, u32[]{:S(2)}) collective-permute-start(bf16[70,3,256]{2,1,0:T(4,128)(2,1)S(1)} %get-tuple-element.69), channel_id=1, source_target_pairs={{0,1},{1,2},{2,3},{3,4},{4,5},{5,6},{6,7},{7,8},{8,9},{9,10},{10,1... | collective-permute-start | bytes 322568 | tf_op jit(solution)/shard_map/ppermute | solution.py:18
  305.5 7.9 %collective-permute-start.7 = (bf16[70,3,256]{2,1,0:T(4,128)(2,1)S(1)}, bf16[70,3,256]{2,1,0:T(4,128)(2,1)S(1)}, u32[]{:S(2)}, u32[]{:S(2)}) collective-permute-start(bf16[70,3,256]{2,1,0:T(4,128)(2,1)S(1)} %get-tuple-element.70), channel_id=1, source_target_pairs={{1,0},{2,1},{3,2},{4,3},{5,4},{6,5},{7,6},{8,7},{9,8},{10,9},{11,1... | collective-permute-start | bytes 322568 | tf_op jit(solution)/shard_map/ppermute | solution.py:21
Sparse Core Ops, SparseCore 0:
  133.8 158.2 all-reduce.6
  317.0 144.7 all-reduce.4
